TPU v7x, 128 devices: a whole 4x4x4 slice. The times are simulated.
128 devices in a mesh: row: 16 (over y_hi, z, core), col: 8 (over x, y_lo).
Axes of the slice: x: 4, y: 4 (y_hi: 2, y_lo: 2; y = y_hi * 2 + y_lo), z: 4, core: 2. Of those that a mesh axis runs over, the one named last changes fastest.
Arguments:
- query: bfloat16 [384, 1024, 128], P('row', 'col'), may hold values from -12 to 12
- key: bfloat16 [384, 1024, 128], P('row', 'col'), may hold values from -6 to 6
- value: bfloat16 [384, 1024, 128], P('row', 'col'), may hold values from -6 to 6
- gate: bfloat16 [384, 1024, 128], P('row', 'col'), may hold values from -6 to 6
- d_out: bfloat16 [384, 1024, 128], P('row', 'col'), may hold values from -6 to 6
- bias: bfloat16 [4, 1024, 1024], P(None, 'col'), may hold values from -6 to 6
- length: int32 [1], replicated, may hold values from 513 to 1024
Outputs:
- d_query: bfloat16 [384, 1024, 128], P('row', 'col')
- d_key: bfloat16 [384, 1024, 128], P('row', 'col')
- d_value: bfloat16 [384, 1024, 128], P('row', 'col')
- d_gate: bfloat16 [384, 1024, 128], P('row', 'col')
- d_bias: float32 [4, 1024, 1024], P(None, 'row', 'col')
All inputs are finite; a program needn't handle non-finite values.
Results may differ from a plain program's by a relative error of at most 0.014.
Values may be sent and summed in bfloat16 or wider, within the bound.
A program may use at most 128 MiB of HBM per device.

v0:
```python
import jax
import jax.numpy as jnp
from jax import lax
from jax.sharding import PartitionSpec as P

N = 1024
HEADS = 4
HEAD_DIM = 32
GROUP = 4


def block_backward(query_block, key_block, value_block, gate_block, dout_block, bias_f, key_valid):
    row_count, col_count, channels = query_block.shape
    key_count = key_block.shape[1]
    scaling = HEAD_DIM ** (-0.5)
    q_heads = query_block.reshape(row_count, col_count, HEADS, HEAD_DIM)
    k_heads = key_block.reshape(row_count, key_count, HEADS, HEAD_DIM)
    v_heads = value_block.reshape(row_count, key_count, HEADS, HEAD_DIM)
    logits = (
        jnp.einsum("ijhc,ikhc->ihjk", q_heads, k_heads, preferred_element_type=jnp.float32)
        * scaling
        + bias_f[None]
    )
    logits = jnp.where(key_valid, logits, -1e30)
    row_max = jnp.max(logits, axis=-1, keepdims=True)
    exponent = jnp.where(key_valid, jnp.exp(logits - row_max), 0.0)
    weights = exponent / jnp.sum(exponent, axis=-1, keepdims=True)
    weights_bf = weights.astype(jnp.bfloat16)
    attended = jnp.einsum(
        "ihjk,ikhc->ijhc", weights_bf, v_heads, preferred_element_type=jnp.float32
    )
    gate_sig = jax.nn.sigmoid(
        gate_block.reshape(row_count, col_count, HEADS, HEAD_DIM).astype(jnp.float32)
    )
    upstream = dout_block.reshape(row_count, col_count, HEADS, HEAD_DIM).astype(jnp.float32)
    gate_grad = (upstream * attended * gate_sig * (1.0 - gate_sig)).astype(jnp.bfloat16)
    grad_att = upstream * gate_sig
    row_dot = jnp.sum(grad_att * attended, axis=-1)
    grad_att_bf = grad_att.astype(jnp.bfloat16)
    grad_weight = jnp.einsum(
        "ijhc,ikhc->ihjk", grad_att_bf, v_heads, preferred_element_type=jnp.float32
    )
    grad_logits = weights * (grad_weight - jnp.transpose(row_dot, (0, 2, 1))[..., None])
    grad_logits_bf = grad_logits.astype(jnp.bfloat16)
    query_grad = (
        jnp.einsum("ihjk,ikhc->ijhc", grad_logits_bf, k_heads, preferred_element_type=jnp.float32)
        * scaling
    )
    key_term = (
        jnp.einsum("ihjk,ijhc->ikhc", grad_logits_bf, q_heads, preferred_element_type=jnp.float32)
        * scaling
    )
    value_term = jnp.einsum(
        "ihjk,ijhc->ikhc", weights_bf, grad_att_bf, preferred_element_type=jnp.float32
    )
    bias_term = jnp.sum(grad_logits, axis=0)
    return (
        query_grad.astype(jnp.bfloat16).reshape(row_count, col_count, channels),
        gate_grad.reshape(row_count, col_count, channels),
        key_term.astype(jnp.bfloat16).reshape(row_count, key_count, channels),
        value_term.astype(jnp.bfloat16).reshape(row_count, key_count, channels),
        bias_term,
    )


def on_device(query, key, value, gate, d_out, bias, length):
    row_count, col_count, channels = query.shape
    blocks = row_count // GROUP
    key_valid = jnp.arange(N) < length[0]
    bias_f = bias.astype(jnp.float32)

    def split(array):
        return array.reshape(blocks, GROUP, array.shape[1], array.shape[2])

    keys_all, values_all = (
        lax.all_gather(key, "col", axis=1, tiled=True),
        lax.all_gather(value, "col", axis=1, tiled=True),
    )
    key_blocks, value_blocks = (split(keys_all), split(values_all))

    def one_block(bias_sum, pieces):
        query_block, gate_block, dout_block, key_block, value_block = pieces
        query_grad, gate_grad, key_term, value_term, bias_term = block_backward(
            query_block, key_block, value_block, gate_block, dout_block, bias_f, key_valid
        )
        key_out, value_out = (key_term, value_term)
        return (bias_sum + bias_term, (query_grad, gate_grad, key_out, value_out))

    start = jnp.zeros((HEADS, col_count, N), jnp.float32)
    bias_sum, stacked = lax.scan(
        one_block, start, (split(query), split(gate), split(d_out), key_blocks, value_blocks)
    )
    query_grad = stacked[0].reshape(row_count, col_count, channels)
    gate_grad = stacked[1].reshape(row_count, col_count, channels)
    key_terms = stacked[2].reshape(row_count, N, channels)
    value_terms = stacked[3].reshape(row_count, N, channels)
    key_sum, value_sum = (
        lax.psum_scatter(key_terms, "col", scatter_dimension=1, tiled=True).astype(jnp.float32),
        lax.psum_scatter(value_terms, "col", scatter_dimension=1, tiled=True).astype(jnp.float32),
    )
    key_grad, value_grad = (key_sum.astype(jnp.bfloat16), value_sum.astype(jnp.bfloat16))
    moved = lax.all_to_all(
        bias_sum.astype(jnp.bfloat16), "col", split_axis=2, concat_axis=1, tiled=True
    ).astype(bias_sum.dtype)
    bias_grad = lax.psum_scatter(
        moved.astype(jnp.bfloat16), "row", scatter_dimension=1, tiled=True
    ).astype(jnp.float32)
    return (query_grad, key_grad, value_grad, gate_grad, bias_grad)


def solution(mesh):
    in_specs = (
        P("row", "col", None),
        P("row", "col", None),
        P("row", "col", None),
        P("row", "col", None),
        P("row", "col", None),
        P(None, "col", None),
        P(),
    )
    out_specs = (
        P("row", "col", None),
        P("row", "col", None),
        P("row", "col", None),
        P("row", "col", None),
        P(None, "row", "col"),
    )
    return jax.shard_map(
        on_device, mesh=mesh, in_specs=in_specs, out_specs=out_specs, check_vma=False
    )
```

profile of v0, /device:TPU:1, one launch (start us, length us, event | category | flops | bytes accessed | tf_op | source)
XLA Modules:
  0.0 886.6 jit_solution(9511931417677891806)
XLA Ops:
  8.8 2.3 copy.22
  11.0 2.3 copy.25
  13.3 2.3 copy.24
  17.2 124.5 %all-gather.3.cloned.1.call-done = bf16[24,1024,128]{2,1,0:T(8,128)(2,1)} async-done(((bf16[24,128,128]{2,1,0:T(8,128)(2,1)}), bf16[24,1024,128]{2,1,0:T(8,128)(2,1)}) %all-gather.3.cloned.1.call-update) | async-done | bytes 6291472 | tf_op jit(solution)/shard_map/all_gather | solution.py:76
  141.7 8.6 copy.23
  150.3 123.4 %all-gather.5.cloned.1.call-done = bf16[24,1024,128]{2,1,0:T(8,128)(2,1)} async-done(((bf16[24,128,128]{2,1,0:T(8,128)(2,1)}), bf16[24,1024,128]{2,1,0:T(8,128)(2,1)}) %all-gather.5.cloned.1.call-update) | async-done | bytes 6291472 | tf_op jit(solution)/shard_map/all_gather | solution.py:77
  273.7 8.7 copy.26
  282.4 241.8 %while.19 = (s32[]{:T(128)}, f32[4,128,1024]{2,1,0:T(8,128)}, bf16[6,4,128,128]{3,2,1,0:T(8,128)(2,1)}, bf16[6,4,128,128]{3,2,1,0:T(8,128)(2,1)}, bf16[6,4,1024,...) while((s32[]{:T(128)}, f32[4,128,1024]{2,1,0:T(8,128)}, ...), condition=%wide.region_5.6_spmd.clone, body=%wide.region_0.5_spmd.clone.sunk | while | flops 836042752 | bytes 101755184 | solution.py:90
  288.5 7.0 fusion.72
  295.6 4.0 fusion.73
  299.6 2.2 fusion.74
  305.0 4.8 fusion.75
  315.6 2.9 multiply_convert_fusion.2
  327.5 7.0 fusion.72
  334.5 4.0 fusion.73
  338.6 2.2 fusion.74
  344.0 4.8 fusion.75
  352.2 3.6 select_add_fusion.2
  356.1 2.9 multiply_convert_fusion.2
  368.1 7.0 fusion.72
  375.1 4.0 fusion.73
  379.1 2.2 fusion.74
  384.6 4.8 fusion.75
  392.8 3.6 select_add_fusion.2
  396.7 2.9 multiply_convert_fusion.2
  408.6 7.0 fusion.72
  415.7 4.0 fusion.73
  419.7 2.2 fusion.74
  425.2 4.8 fusion.75
  433.4 3.6 select_add_fusion.2
  437.3 2.9 multiply_convert_fusion.2
  449.2 7.0 fusion.72
  456.2 4.0 fusion.73
  460.2 2.2 fusion.74
  465.7 4.8 fusion.75
  473.9 3.6 select_add_fusion.2
  477.8 2.9 multiply_convert_fusion.2
  489.8 7.0 fusion.72
  496.8 4.0 fusion.73
  500.8 2.2 fusion.74
  506.3 4.8 fusion.75
  514.5 3.6 select_add_fusion.2
  518.4 2.9 multiply_convert_fusion.2
  524.1 2.1 copy.31
  526.2 18.8 %all_to_all.18 = bf16[4,128,1024]{1,0,2:T(4,128)(2,1)S(1)} all-to-all(bf16[4,128,1024]{1,0,2:T(4,128)(2,1)S(1)} %copy.31), channel_id=1, replica_groups=mesh['row'=16,'col'=8] {'col'}, dimensions={2} | all-to-all | bytes 2097152 | tf_op jit(solution)/shard_map/all_to_all | solution.py:102
  547.6 65.5 %reduce-scatter.8.cloned.1.call-done = bf16[4,64,128]{2,1,0:T(8,128)(2,1)} async-done(((bf16[4,1024,128]{2,1,0:T(8,128)(2,1)}), bf16[4,64,128]{2,1,0:T(8,128)(2,1)}) %reduce-scatter.8.cloned.1.call-update) | async-done | bytes 65552 | tf_op jit(solution)/shard_map/reduce_scatter | solution.py:105
  614.6 131.9 %reduce-scatter.6.cloned.1.call-done = bf16[24,128,128]{2,1,0:T(8,128)(2,1)} async-done(((bf16[24,1024,128]{2,1,0:T(8,128)(2,1)}), bf16[24,128,128]{2,1,0:T(8,128)(2,1)}) %reduce-scatter.6.cloned.1.call-update) | async-done | bytes 786448 | tf_op jit(solution)/shard_map/reduce_scatter | solution.py:99
  746.5 133.5 %reduce-scatter.4.cloned.1.call-done = bf16[24,128,128]{2,1,0:T(8,128)(2,1)} async-done(((bf16[24,1024,128]{2,1,0:T(8,128)(2,1)}), bf16[24,128,128]{2,1,0:T(8,128)(2,1)}) %reduce-scatter.4.cloned.1.call-update) | async-done | bytes 786448 | tf_op jit(solution)/shard_map/reduce_scatter | solution.py:98
  (153 shorter events, 105.0 us)
Async XLA Ops:
  7.2 8.4 copy-start.4
  7.2 134.5 %all-gather.3.cloned.1.call-start = ((), (), s32[]{:S(2)}) async-start(), calls=%async_computation.4 | async-start | bytes 7077888 | tf_op jit(solution)/shard_map/all_gather | solution.py:76
  7.9 265.8 %all-gather.5.cloned.1.call-start = ((), (), s32[]{:S(2)}) async-start(), calls=%async_computation.5 | async-start | bytes 7077888 | tf_op jit(solution)/shard_map/all_gather | solution.py:77
  8.7 604.5 %reduce-scatter.8.cloned.1.call-start = ((), (), s32[]{:S(2)}) async-start(), calls=%async_computation.8 | async-start | bytes 1114112 | tf_op jit(solution)/shard_map/reduce_scatter | solution.py:105
  284.9 10.7 %copy-start.2 = (bf16[1,4,128,128]{2,3,1,0:T(8,128)(2,1)}, bf16[1,4,128,128]{2,3,1,0:T(8,128)(2,1)S(1)}, u32[]{:S(2)}) copy-start(bf16[1,4,128,128]{2,3,1,0:T(8,128)(2,1)S(1)} %constant_dynamic-slice_fusion.10) | copy-start | bytes 393220 | tf_op jit(solution)/shard_map/while
  309.8 1.9 copy-start
  309.8 5.6 copy-start.1
  309.8 5.7 copy-start.3
  323.8 10.7 %copy-start.2 = (bf16[1,4,128,128]{2,3,1,0:T(8,128)(2,1)}, bf16[1,4,128,128]{2,3,1,0:T(8,128)(2,1)S(1)}, u32[]{:S(2)}) copy-start(bf16[1,4,128,128]{2,3,1,0:T(8,128)(2,1)S(1)} %constant_dynamic-slice_fusion.10) | copy-start | bytes 393220 | tf_op jit(solution)/shard_map/while
  348.8 1.9 copy-start
  348.8 7.2 copy-start.1
  348.8 7.3 copy-start.3
  364.4 10.7 %copy-start.2 = (bf16[1,4,128,128]{2,3,1,0:T(8,128)(2,1)}, bf16[1,4,128,128]{2,3,1,0:T(8,128)(2,1)S(1)}, u32[]{:S(2)}) copy-start(bf16[1,4,128,128]{2,3,1,0:T(8,128)(2,1)S(1)} %constant_dynamic-slice_fusion.10) | copy-start | bytes 393220 | tf_op jit(solution)/shard_map/while
  389.4 1.9 copy-start
  389.4 7.2 copy-start.1
  389.4 7.3 copy-start.3
  405.0 10.7 %copy-start.2 = (bf16[1,4,128,128]{2,3,1,0:T(8,128)(2,1)}, bf16[1,4,128,128]{2,3,1,0:T(8,128)(2,1)S(1)}, u32[]{:S(2)}) copy-start(bf16[1,4,128,128]{2,3,1,0:T(8,128)(2,1)S(1)} %constant_dynamic-slice_fusion.10) | copy-start | bytes 393220 | tf_op jit(solution)/shard_map/while
  429.9 1.9 copy-start
  430.0 7.2 copy-start.1
  430.0 7.3 copy-start.3
  445.5 10.7 %copy-start.2 = (bf16[1,4,128,128]{2,3,1,0:T(8,128)(2,1)}, bf16[1,4,128,128]{2,3,1,0:T(8,128)(2,1)S(1)}, u32[]{:S(2)}) copy-start(bf16[1,4,128,128]{2,3,1,0:T(8,128)(2,1)S(1)} %constant_dynamic-slice_fusion.10) | copy-start | bytes 393220 | tf_op jit(solution)/shard_map/while
  470.5 1.9 copy-start
  470.5 7.2 copy-start.1
  470.5 7.3 copy-start.3
  486.1 10.7 %copy-start.2 = (bf16[1,4,128,128]{2,3,1,0:T(8,128)(2,1)}, bf16[1,4,128,128]{2,3,1,0:T(8,128)(2,1)S(1)}, u32[]{:S(2)}) copy-start(bf16[1,4,128,128]{2,3,1,0:T(8,128)(2,1)S(1)} %constant_dynamic-slice_fusion.10) | copy-start | bytes 393220 | tf_op jit(solution)/shard_map/while
  511.1 1.9 copy-start
  511.1 7.2 copy-start.1
  511.1 7.3 copy-start.3
  546.4 200.1 %reduce-scatter.6.cloned.1.call-start = ((), (), s32[]{:S(2)}) async-start(), calls=%async_computation.7 | async-start | bytes 7077888 | tf_op jit(solution)/shard_map/reduce_scatter | solution.py:99
  547.0 333.0 %reduce-scatter.4.cloned.1.call-start = ((), (), s32[]{:S(2)}) async-start(), calls=%async_computation.6 | async-start | bytes 7077888 | tf_op jit(solution)/shard_map/reduce_scatter | solution.py:98
Sparse Core Ops, SparseCore 0:
  9.6 132.0 all-gather.2
  143.3 130.3 all-gather.4
  546.6 66.5 reduce-scatter.7
  616.0 130.5 reduce-scatter.5
  749.4 130.6 reduce-scatter.3
where the time goes:
time: 889 us; the launch traced here: 887 us
  waiting for transfers between devices  581 us (65%)
  matrix products  120 us (13%)
  local copies, waits for them, and re-layouts  94.3 us (11%)
  other arithmetic  57.2 us (6%)
  blocking collectives  18.8 us (2%)
  between operations  13.8 us (2%)
    reduce_scatter x1, waiting for transfers between devices, on_device(): lax.psum_scatter(key_terms, 'col', scatter_dimension=1, tiled=True)  134 us
    reduce_scatter x1, waiting for transfers between devices, on_device(): lax.psum_scatter(value_terms, 'col', scatter_dimension=1, tiled=True)  132 us
    all_gather x1, waiting for transfers between devices, on_device(): lax.all_gather(key, 'col', axis=1, tiled=True)  124 us
    all_gather x1, waiting for transfers between devices, on_device(): lax.all_gather(value, 'col', axis=1, tiled=True)  123 us
    reduce_scatter x1, waiting for transfers between devices, on_device(): lax.psum_scatter(moved.astype(jnp.bfloat16), 'row', scatter_dimension=1,...  65.5 us
    sub x6, matrix products, block_backward(): exponent = jnp.where(key_valid, jnp.exp(logits - row_max), 0.0)  42.3 us
    dot_general x6, matrix products, block_backward(): jnp.einsum('ijhc,ikhc->ihjk', grad_att_bf, v_heads, preferred_element_typ...  28.6 us
    dynamic_update_slice x36, local copies, waits for them, and re-layouts, on_device(): lax.scan(one_block, start, (split(query), split(gate), split(d_out), key_...  28.5 us
  transfers between devices with their start and end apart: 5, of which 5 were waited for; matrix products, arithmetic and copies ran while one was open for 2% of the time, Pallas kernels for 0%

commit v1 on v0

v1 whole, which is shorter than its diff:
```python
import functools
import math

import jax
import jax.numpy as jnp
from jax import lax
from jax.experimental import pallas as pl
from jax.experimental.pallas import tpu as pltpu
from jax.sharding import PartitionSpec as P

MESH = pl.DeviceIdType.MESH
BF = jnp.bfloat16
F32 = jnp.float32
HEADS = 4
C = 32
SCALE = C**-0.5
LOG2E = math.log2(math.e)
CI = 2
KC = 256
NN = (((1,), (0,)), ((), ()))
NT = (((1,), (1,)), ((), ()))


def dot(a, b, dims=NN):
    return lax.dot_general(a, b, dims, preferred_element_type=F32)


def sigmoid(x):
    return 1.0 / (1.0 + jnp.exp(-x))


def compute_row(qt, gat, kt, vt, bt_ref, d_ref, s_ref, e_ref, ds_ref, k2_ref, v1_ref):
    n = kt.shape[1]
    width = qt.shape[1]
    k2_ref[...] = jnp.concatenate([kt, kt], axis=0).T
    v1t = jnp.concatenate([vt, jnp.ones((16, n), BF)], axis=0)
    v1_ref[...] = v1t.T
    row = lax.broadcasted_iota(jnp.int32, (16, width), 0)
    q = qt.astype(F32) * (SCALE * LOG2E)
    q_hi = q.astype(BF)
    q_lo = (q - q_hi.astype(F32)).astype(BF)
    q2 = jnp.concatenate([q_hi, q_lo], axis=0)
    peak = None
    for c in range(n // KC):
        ks = slice(c * KC, (c + 1) * KC)
        s = dot(k2_ref[ks, :], q2) + bt_ref[ks, :]
        s_ref[ks, :] = s
        part = jnp.max(s.reshape(KC // 8, 8, width), axis=0)
        peak = part if peak is None else jnp.maximum(peak, part)
    peak = jnp.max(peak, axis=0, keepdims=True)
    for c in range(n // KC):
        ks = slice(c * KC, (c + 1) * KC)
        e = jnp.exp2(s_ref[ks, :] - peak)
        s_ref[ks, :] = e
        e_ref[ks, :] = e.astype(BF)
    summed = dot(v1t, e_ref[...])
    inv = 1.0 / summed[C : C + 1, :]
    att = summed[:C, :] * inv
    ga = gat.astype(F32)
    row_dot = jnp.sum(ga * att, axis=0, keepdims=True) * inv
    ga_n = (ga * inv).astype(BF)
    r_hi = row_dot.astype(BF).astype(F32)
    r_lo = row_dot - r_hi
    ext = jnp.where(row == 0, -r_hi, jnp.where(row == 1, -r_lo, 0.0)).astype(BF)
    g1 = jnp.concatenate([ga_n, ext], axis=0)
    for c in range(n // KC):
        ks = slice(c * KC, (c + 1) * KC)
        ds = dot(v1_ref[ks, :], g1) * s_ref[ks, :]
        d_ref[ks, :] += ds
        ds_ref[ks, :] = ds.astype(BF)
    dq = dot(kt, ds_ref[...]) * SCALE
    dk = dot(qt, ds_ref[...], NT) * SCALE
    dv = dot(ga_n, e_ref[...], NT)
    return dq, att, dk, dv


def kernel(
    q, k, v, g, do, bias, length,
    dq, dk, dv, dg, db,
    snd, rx, ry, dkv, ryd, outs, fin,
    bts, btr, bt, dacc, s_ref, e_ref, ds_ref, k2_ref, v1_ref,
    dt, t1s, t1r, t2s, t2u, t3r, t4s, t4r,
    s1, r1, s2, r2, s4, r4, s5, r5, sb, rb, st, rt,
):
    r, c = lax.axis_index("row"), lax.axis_index("col")
    yh, z, core = lax.div(r, 8), lax.rem(lax.div(r, 2), 4), lax.rem(r, 2)
    x, yl = lax.div(c, 2), lax.rem(c, 2)
    rows = q.shape[0]
    chunks = rows // CI
    xs = [lax.rem(x + d, 4) for d in (1, 2, 3)]
    x_ids = [(r, t * 2 + yl) for t in xs]
    y_id = (r, x * 2 + 1 - yl)
    core_id = (r + 1 - 2 * core, c)
    peers = []
    for dyh in (0, 1):
        for dz in range(4):
            if dyh or dz:
                yh2 = yh if dyh == 0 else 1 - yh
                peers.append((yh2, lax.rem(z + dz, 4)))
    peer_ids = [(a * 8 + b * 2 + core, c) for a, b in peers]

    everyone = x_ids + [y_id, core_id] + peer_ids
    barrier = pltpu.get_barrier_semaphore()
    for one in everyone:
        pl.semaphore_signal(barrier, inc=1, device_id=one, device_id_type=MESH)

    def copy(src, dst, send, recv, to):
        return pltpu.make_async_remote_copy(
            src_ref=src, dst_ref=dst, send_sem=send, recv_sem=recv, device_id=to, device_id_type=MESH
        )

    def in_copy(n, d):
        i = pl.ds(n * CI, CI)
        return copy(snd.at[i, xs[d]], rx.at[i, x], s1.at[n, d], r1.at[n, d], x_ids[d])

    def y_copy(n):
        i = pl.ds(n * CI, CI)
        return copy(rx.at[i, :, pl.ds(2, 2)], ry.at[i], s2.at[n], r2.at[n], y_id)

    def back_copy(n):
        i = pl.ds(n * CI, CI)
        return copy(dkv.at[i, 1], ryd.at[i], s4.at[n], r4.at[n], y_id)

    def out_copy(n, d):
        i = pl.ds(n * CI, CI)
        return copy(outs.at[i, xs[d]], fin.at[i, x], s5.at[n, d], r5.at[n, d], x_ids[d])

    def bias_copy(d):
        return copy(bts.at[xs[d]], btr.at[x], sb.at[d], rb.at[d], x_ids[d])

    def prepare(n):
        for one in range(CI):
            i = n * CI + one
            ga = do[i].astype(F32) * sigmoid(g[i].astype(F32))
            for t, array in enumerate((q[i], ga.astype(BF), k[i], v[i])):
                snd[i, :, t] = array.T.reshape(HEADS, C, 128)
            rx[i, x] = snd[i, x]

    prepare(0)
    pl.semaphore_wait(barrier, len(everyone))
    for d in range(3):
        in_copy(0, d).start()

    def bias_head(h, _):
        for p in range(2):
            for b in range(4):
                at = pl.multiple_of((2 * b + (yl if p == 0 else 1 - yl)) * 128, 128)
                bts[h, pl.ds((p * 4 + b) * 128, 128), :] = bias[h, :, pl.ds(at, 128)].T
        return 0

    lax.fori_loop(0, HEADS, bias_head, 0)
    for d in range(3):
        bias_copy(d).start()
    btr[x] = bts[x]

    def prepare_and_send(n, _):
        prepare(n)
        for d in range(3):
            in_copy(n, d).start()
        return 0

    lax.fori_loop(1, chunks, prepare_and_send, 0)

    dacc[...] = jnp.zeros_like(dacc)
    for d in range(3):
        in_copy(0, d).wait_recv()
    y_copy(0).start()
    for d in range(3):
        bias_copy(d).wait_recv()
    valid = length[0]
    for p in range(2):
        for b in range(4):
            first = (2 * b + (yl if p == 0 else 1 - yl)) * 128
            ks = pl.ds((p * 4 + b) * 128, 128)
            live = lax.broadcasted_iota(jnp.int32, (128, 128), 0) + first < valid
            for t in range(4):
                bt[ks, pl.ds(t * 128, 128)] = jnp.where(live, btr[t, ks, :].astype(F32) * LOG2E, -1e30)

    def compute(n):
        def one(j, _):
            i = n * CI + j
            qt = jnp.concatenate([rx[i, t, 0] for t in range(4)], axis=1)
            gat = jnp.concatenate([rx[i, t, 1] for t in range(4)], axis=1)
            kt = jnp.concatenate([rx[i, t, 2] for t in range(4)] + [ry[i, t, 0] for t in range(4)], axis=1)
            vt = jnp.concatenate([rx[i, t, 3] for t in range(4)] + [ry[i, t, 1] for t in range(4)], axis=1)
            a, b, e, f = compute_row(qt, gat, kt, vt, bt, dacc, s_ref, e_ref, ds_ref, k2_ref, v1_ref)
            for t in range(4):
                js = slice(t * 128, t * 128 + 128)
                outs[i, t, 0] = a[:, js].astype(BF)
                outs[i, t, 1] = b[:, js].astype(BF)
                for p in range(2):
                    ks = slice((p * 4 + t) * 128, (p * 4 + t) * 128 + 128)
                    dkv[i, p, t, 0] = e[:, ks].astype(BF)
                    dkv[i, p, t, 1] = f[:, ks].astype(BF)
            return 0

        lax.fori_loop(0, CI, one, 0)

    def add_and_send(n):
        back_copy(n).wait_recv()
        for one in range(CI):
            i = n * CI + one
            total = dkv[i, 0].astype(F32) + ryd[i].astype(F32)
            outs[i, :, pl.ds(2, 2)] = total.astype(BF)
            fin[i, x] = outs[i, x]
        for d in range(3):
            out_copy(n, d).start()

    def finish(n):
        for d in range(3):
            out_copy(n, d).wait_recv()
        for one in range(CI):
            i = n * CI + one
            dq[i] = fin[i, :, 0].reshape(128, 128).T
            dk[i] = fin[i, :, 2].reshape(128, 128).T
            dv[i] = fin[i, :, 3].reshape(128, 128).T
            att = fin[i, :, 1].reshape(128, 128).T.astype(F32)
            s = sigmoid(g[i].astype(F32))
            dg[i] = (do[i].astype(F32) * att * s * (1.0 - s)).astype(BF)

    def step(n, _):
        @pl.when(n + 1 < chunks)
        def _():
            for d in range(3):
                in_copy(n + 1, d).wait_recv()
            y_copy(n + 1).start()

        y_copy(n).wait_recv()
        compute(n)
        back_copy(n).start()

        @pl.when(n >= 1)
        def _():
            add_and_send(n - 1)

        @pl.when(n >= 2)
        def _():
            finish(n - 2)

        return 0

    lax.fori_loop(0, chunks, step, 0)

    for t in range(4):
        for b in range(8):
            dt[pl.ds(t * 128, 128), pl.ds(b * 128, 128)] = dacc[pl.ds(b * 128, 128), pl.ds(t * 128, 128)].T
    for t in range(4):
        t1s[t] = dt[pl.ds(pl.multiple_of(t * 128 + 64 * (1 - core), 64), 64), :].astype(BF)
    one = copy(t1s, t1r, st.at[0], rt.at[0], core_id)
    one.start()
    add_and_send(chunks - 1)
    one.wait_recv()
    for t in range(4):
        total = dt[pl.ds(pl.multiple_of(t * 128 + 64 * core, 64), 64), :] + t1r[t].astype(F32)
        t2u[yl, t] = total[:, :512].astype(BF)
        t2s[t] = total[:, 512:].astype(BF)
    two = copy(t2s, t2u.at[yl], st.at[1], rt.at[1], y_id)
    two.start()
    finish(chunks - 2)
    two.wait_recv()
    me = yh * 4 + z
    three = []
    for d, (a, b) in enumerate(peers):
        src = t2u.at[lax.rem(b, 2), 2 * a + lax.div(b, 2)]
        three.append(copy(src, t3r.at[me], st.at[2 + d], rt.at[2 + d], peer_ids[d]))
        three[-1].start()
    t3r[me] = t2u[lax.rem(z, 2), 2 * yh + lax.div(z, 2)]
    finish(chunks - 1)
    for one_copy in three:
        one_copy.wait_recv()
    total = t3r[0].astype(F32)
    for s in range(1, 8):
        total += t3r[s].astype(F32)
    for t in range(4):
        t4s[t] = total[:, t * 128 : t * 128 + 128].astype(BF)
    four = []
    for d in range(3):
        four.append(copy(t4s.at[xs[d]], t4r.at[x], st.at[9 + d], rt.at[9 + d], x_ids[d]))
        four[-1].start()
    t4r[x] = t4s[x]
    for one_copy in four:
        one_copy.wait_recv()
    for h in range(HEADS):
        db[h] = t4r[h].astype(F32)

    def drain(n, _):
        for d in range(3):
            in_copy(n, d).wait_send()
            out_copy(n, d).wait_send()
        y_copy(n).wait_send()
        back_copy(n).wait_send()
        return 0

    lax.fori_loop(0, chunks, drain, 0)
    for d in range(3):
        bias_copy(d).wait_send()
    for one_copy in [one, two] + three + four:
        one_copy.wait_send()


def on_device(query, key, value, gate, d_out, bias, length):
    rows = query.shape[0]
    chunks = rows // CI
    vmem = pl.BlockSpec(memory_space=pltpu.VMEM)
    pair = jax.ShapeDtypeStruct(query.shape, BF)
    dma = pltpu.SemaphoreType.DMA
    out = pl.pallas_call(
        kernel,
        out_shape=[pair, pair, pair, pair, jax.ShapeDtypeStruct((HEADS, 64, 128), F32)],
        in_specs=[vmem] * 6 + [pl.BlockSpec(memory_space=pltpu.SMEM)],
        out_specs=[vmem] * 5,
        scratch_shapes=[
            pltpu.VMEM((rows, 4, 4, C, 128), BF),
            pltpu.VMEM((rows, 4, 4, C, 128), BF),
            pltpu.VMEM((rows, 4, 2, C, 128), BF),
            pltpu.VMEM((rows, 2, 4, 2, C, 128), BF),
            pltpu.VMEM((rows, 4, 2, C, 128), BF),
            pltpu.VMEM((rows, 4, 4, C, 128), BF),
            pltpu.VMEM((rows, 4, 4, C, 128), BF),
            pltpu.VMEM((4, 1024, 128), BF),
            pltpu.VMEM((4, 1024, 128), BF),
            pltpu.VMEM((1024, 512), F32),
            pltpu.VMEM((1024, 512), F32),
            pltpu.VMEM((1024, 512), F32),
            pltpu.VMEM((1024, 512), BF),
            pltpu.VMEM((1024, 512), BF),
            pltpu.VMEM((1024, 64), BF),
            pltpu.VMEM((1024, 48), BF),
            pltpu.VMEM((512, 1024), F32),
            pltpu.VMEM((4, 64, 1024), BF),
            pltpu.VMEM((4, 64, 1024), BF),
            pltpu.VMEM((4, 64, 512), BF),
            pltpu.VMEM((2, 4, 64, 512), BF),
            pltpu.VMEM((8, 64, 512), BF),
            pltpu.VMEM((4, 64, 128), BF),
            pltpu.VMEM((4, 64, 128), BF),
            dma((chunks, 3)), dma((chunks, 3)),
            dma((chunks,)), dma((chunks,)),
            dma((chunks,)), dma((chunks,)),
            dma((chunks, 3)), dma((chunks, 3)),
            dma((3,)), dma((3,)),
            dma((12,)), dma((12,)),
        ],
        compiler_params=pltpu.CompilerParams(
            collective_id=0, has_side_effects=True, vmem_limit_bytes=60 * 2**20
        ),
    )(query, key, value, gate, d_out, bias, length)
    return tuple(out)


def solution(mesh):
    pair = P("row", "col", None)
    return jax.shard_map(
        on_device,
        mesh=mesh,
        in_specs=(pair,) * 5 + (P(None, "col", None), P()),
        out_specs=(pair,) * 4 + (P(None, "row", "col"),),
        check_vma=False,
    )
```

time: 889 us -> 146 us (0.16)
  waiting for transfers between devices: 581 us -> 0 us
  Pallas kernels: 0 us -> 136 us
  matrix products: 120 us -> 0 us
  local copies, waits for them, and re-layouts: 94.3 us -> 6.67 us
  other arithmetic: 57.2 us -> 0 us
  blocking collectives: 18.8 us -> 0 us
  between operations: 13.8 us -> 1.3 us
    reduce_scatter x3 -> x0, waiting for transfers between devices: 331 us -> none  [the longest x1 134 us: on_device(): lax.psum_scatter(key_terms, 'col', scatter_dimension=1, tiled=True)]
    all_gather x2 -> x0, waiting for transfers between devices: 248 us -> none  [the longest x1 124 us: on_device(): lax.all_gather(key, 'col', axis=1, tiled=True)]
    pallas_call x0 -> x1, Pallas kernels: none -> 136 us  [on_device(): pl.pallas_call(kernel, out_shape=[pair, pair, pair, pair, jax.ShapeDtypeS...]
    dot_general x30 -> x0, matrix products: 78 us -> none  [the longest x6 28.6 us: block_backward(): jnp.einsum('ijhc,ikhc->ihjk', grad_att_bf, v_heads, preferred_element_typ...]
    sub x6 -> x0, matrix products: 42.3 us -> none  [block_backward(): exponent = jnp.where(key_valid, jnp.exp(logits - row_max), 0.0)]
    dynamic_update_slice x36 -> x0, local copies, waits for them, and re-layouts: 28.5 us -> none  [on_device(): lax.scan(one_block, start, (split(query), split(gate), split(d_out), key_...]
    convert_element_type x8 -> x0, other arithmetic: 27.1 us -> none  [the longest x6 24 us: block_backward(): weights_bf = weights.astype(jnp.bfloat16)]
    dynamic_slice x24 -> x0, local copies, waits for them, and re-layouts: 26.6 us -> none  [on_device(): lax.scan(one_block, start, (split(query), split(gate), split(d_out), key_...]
  transfers between devices with their start and end apart: 5 -> 0, of which waited for: 5 -> 0; matrix products, arithmetic and copies ran while one was open for 2% -> 0% of each run, Pallas kernels for 0% -> 0%
where the time goes in v1:
time: 146 us; the launch traced here: 144 us
  Pallas kernels  136 us (93%)
  local copies, waits for them, and re-layouts  6.67 us (5%)
    pallas_call x1, Pallas kernels, on_device(): pl.pallas_call(kernel, out_shape=[pair, pair, pair, pair, jax.ShapeDtypeS...  136 us
    unnamed x13, local copies, waits for them, and re-layouts  6.67 us

profile of v1, /device:TPU:1, one launch (start us, length us, event | category | flops | bytes accessed | tf_op | source)
XLA Modules:
  0.0 144.4 jit_solution(15149420803018437124)
XLA Ops:
  1.3 136.4 %shard_map.110 = (bf16[24,128,128]{2,1,0:T(8,128)(2,1)}, bf16[24,128,128]{2,1,0:T(8,128)(2,1)}, bf16[24,128,128]{2,1,0:T(8,128)(2,1)}, bf16[24,128,128]{2,1,0:T(8,128)(2,1)}, f32[4,64,128]{2,1,0:T(8,128)}) custom-call(bf16[24,128,128]{2,1,0:T(8,128)(2,1)} %q.1, bf16[24,128,128]{2,1,0:T(8,128)(2,1)} %k.1, bf16[24,128,128]{2,1,0:T(8,128)(2,1)} %v.1, ...), custom_call_target="tpu_custom_call" | custom-call | tf_op jit(solution)/shard_map/pallas_call | solution.py:307
  137.7 0.0 copy-start.2
  137.7 2.2 %copy.18 = bf16[24,128,128]{2,1,0:T(8,128)(2,1)} copy(bf16[24,128,128]{2,1,0:T(8,128)(2,1)} %get-tuple-element.10) | data formatting | bytes 1572864
  139.9 0.0 copy-done.2
  139.9 0.0 copy-start.1
  139.9 0.9 copy.19
  140.7 0.5 copy-done.1
  141.3 0.0 copy-start
  141.3 0.9 copy.20
  142.2 0.5 copy-done
  142.7 0.0 copy-start.3
  142.7 0.9 copy.21
  143.6 0.1 copy-done.3
  143.7 0.7 copy.22
Async XLA Ops:
  137.7 2.2 %copy-start.2 = (bf16[24,128,128]{2,1,0:T(8,128)(2,1)S(1)}, bf16[24,128,128]{2,1,0:T(8,128)(2,1)}, u32[]{:S(2)}) copy-start(bf16[24,128,128]{2,1,0:T(8,128)(2,1)} %get-tuple-element.11) | copy-start | bytes 2359300
  139.9 1.4 copy-start.1
  141.3 1.4 copy-start
  142.7 1.0 copy-start.3

commit v2 on v1

--- a/solution.py
+++ b/solution.py
@@ -16,6 +16,8 @@
 SCALE = C**-0.5
 LOG2E = math.log2(math.e)
 CI = 2
+LAG = 8
+ADD = 2
 KC = 256
 NN = (((1,), (0,)), ((), ()))
 NT = (((1,), (1,)), ((), ()))
@@ -75,13 +77,23 @@
 
 
 def kernel(
-    q, k, v, g, do, bias, length,
+    q_hbm, k_hbm, v_hbm, g_hbm, do_hbm, bias_hbm, length,
     dq, dk, dv, dg, db,
+    q, k, v, g, do, bias, sl,
     snd, rx, ry, dkv, ryd, outs, fin,
     bts, btr, bt, dacc, s_ref, e_ref, ds_ref, k2_ref, v1_ref,
-    dt, t1s, t1r, t2s, t2u, t3r, t4s, t4r,
+    dt, t1s, t1r, t2s, t3r, t4s, t4r,
     s1, r1, s2, r2, s4, r4, s5, r5, sb, rb, st, rt,
 ):
+    loads = []
+    for part, i in enumerate((pl.ds(0, CI), pl.ds(CI, q.shape[0] - CI))):
+        for t, (far, near) in enumerate(((g_hbm, g), (do_hbm, do), (q_hbm, q), (k_hbm, k), (v_hbm, v))):
+            loads.append(pltpu.make_async_copy(far.at[i], near.at[i], sl.at[part * 6 + t]))
+        if part == 0:
+            loads.append(pltpu.make_async_copy(bias_hbm, bias, sl.at[5]))
+    for one_load in loads:
+        one_load.start()
+
     r, c = lax.axis_index("row"), lax.axis_index("col")
     yh, z, core = lax.div(r, 8), lax.rem(lax.div(r, 2), 4), lax.rem(r, 2)
     x, yl = lax.div(c, 2), lax.rem(c, 2)
@@ -99,10 +111,20 @@
                 peers.append((yh2, lax.rem(z + dz, 4)))
     peer_ids = [(a * 8 + b * 2 + core, c) for a, b in peers]
 
-    everyone = x_ids + [y_id, core_id] + peer_ids
+    swap_row = yh * 8 + (lax.div(z, 2) * 2 + yl) * 2 + core
+    swap_yl = lax.rem(z, 2)
+    swaps = swap_yl != yl
+    last_ids = [(swap_row, t * 2 + swap_yl) for t in xs]
+    twin_id = (swap_row, x * 2 + swap_yl)
+
+    everyone = x_ids + [y_id, core_id] + peer_ids + last_ids
     barrier = pltpu.get_barrier_semaphore()
     for one in everyone:
         pl.semaphore_signal(barrier, inc=1, device_id=one, device_id_type=MESH)
+
+    @pl.when(swaps)
+    def _():
+        pl.semaphore_signal(barrier, inc=1, device_id=twin_id, device_id_type=MESH)
 
     def copy(src, dst, send, recv, to):
         return pltpu.make_async_remote_copy(
@@ -113,9 +135,14 @@
         i = pl.ds(n * CI, CI)
         return copy(snd.at[i, xs[d]], rx.at[i, x], s1.at[n, d], r1.at[n, d], x_ids[d])
 
-    def y_copy(n):
+    def y_copy(n, d):
         i = pl.ds(n * CI, CI)
-        return copy(rx.at[i, :, pl.ds(2, 2)], ry.at[i], s2.at[n], r2.at[n], y_id)
+        t = xs[2 - d]
+        return copy(rx.at[i, t, pl.ds(2, 2)], ry.at[i, t], s2.at[n, d], r2.at[n, d], y_id)
+
+    def y_own(n):
+        i = pl.ds(n * CI, CI)
+        return copy(snd.at[i, x, pl.ds(2, 2)], ry.at[i, x], s2.at[n, 3], r2.at[n, 3], y_id)
 
     def back_copy(n):
         i = pl.ds(n * CI, CI)
@@ -125,8 +152,14 @@
         i = pl.ds(n * CI, CI)
         return copy(outs.at[i, xs[d]], fin.at[i, x], s5.at[n, d], r5.at[n, d], x_ids[d])
 
+    half = pl.ds(core * 512, 512)
+
     def bias_copy(d):
-        return copy(bts.at[xs[d]], btr.at[x], sb.at[d], rb.at[d], x_ids[d])
+        return copy(bts.at[xs[d], half], btr.at[x, half], sb.at[d], rb.at[d], x_ids[d])
+
+    def bias_twin(d):
+        t = btr.at[xs[2 - d], half]
+        return copy(t, t, sb.at[3 + d], rb.at[3 + d], core_id)
 
     def prepare(n):
         for one in range(CI):
@@ -136,10 +169,25 @@
                 snd[i, :, t] = array.T.reshape(HEADS, C, 128)
             rx[i, x] = snd[i, x]
 
+    def send_in(n):
+        for d in range(3):
+            in_copy(n, d).start()
+        y_own(n).start()
+
+    def forward(n, _):
+        for d in range(3):
+            in_copy(n, d).wait_recv()
+            y_copy(n, d).start()
+        return 0
+
+    def forwarded(n):
+        return jnp.minimum(chunks, 2 + n + lax.div(n, 3))
+
+    for one_load in loads[:5]:
+        one_load.wait()
     prepare(0)
-    pl.semaphore_wait(barrier, len(everyone))
-    for d in range(3):
-        in_copy(0, d).start()
+    pl.semaphore_wait(barrier, len(everyone) + lax.rem(z + yl, 2))
+    send_in(0)
 
     def bias_head(h, _):
         for p in range(2):
@@ -148,6 +196,7 @@
                 bts[h, pl.ds((p * 4 + b) * 128, 128), :] = bias[h, :, pl.ds(at, 128)].T
         return 0
 
+    loads[5].wait()
     lax.fori_loop(0, HEADS, bias_head, 0)
     for d in range(3):
         bias_copy(d).start()
@@ -155,18 +204,20 @@
 
     def prepare_and_send(n, _):
         prepare(n)
-        for d in range(3):
-            in_copy(n, d).start()
+        send_in(n)
         return 0
 
+    for one_load in loads[6:]:
+        one_load.wait()
     lax.fori_loop(1, chunks, prepare_and_send, 0)
 
     dacc[...] = jnp.zeros_like(dacc)
-    for d in range(3):
-        in_copy(0, d).wait_recv()
-    y_copy(0).start()
+    forward(0, 0)
     for d in range(3):
         bias_copy(d).wait_recv()
+        bias_twin(d).start()
+    for d in range(3):
+        bias_twin(d).wait_recv()
     valid = length[0]
     for p in range(2):
         for b in range(4):
@@ -218,27 +269,32 @@
             s = sigmoid(g[i].astype(F32))
             dg[i] = (do[i].astype(F32) * att * s * (1.0 - s)).astype(BF)
 
+    def finish_range(low, high):
+        def one(n, _):
+            finish(n)
+            return 0
+
+        lax.fori_loop(low, high, one, 0)
+
     def step(n, _):
-        @pl.when(n + 1 < chunks)
-        def _():
-            for d in range(3):
-                in_copy(n + 1, d).wait_recv()
-            y_copy(n + 1).start()
-
-        y_copy(n).wait_recv()
+        lax.fori_loop(forwarded(n), forwarded(n + 1), forward, 0)
+        for d in range(3):
+            y_copy(n, d).wait_recv()
+        y_own(n).wait_recv()
         compute(n)
         back_copy(n).start()
 
-        @pl.when(n >= 1)
+        @pl.when(n >= ADD)
         def _():
-            add_and_send(n - 1)
-
-        @pl.when(n >= 2)
+            add_and_send(n - ADD)
+
+        @pl.when(n >= LAG)
         def _():
-            finish(n - 2)
+            finish(n - LAG)
 
         return 0
 
+    forward(1, 0)
     lax.fori_loop(0, chunks, step, 0)
 
     for t in range(4):
@@ -248,24 +304,22 @@
         t1s[t] = dt[pl.ds(pl.multiple_of(t * 128 + 64 * (1 - core), 64), 64), :].astype(BF)
     one = copy(t1s, t1r, st.at[0], rt.at[0], core_id)
     one.start()
-    add_and_send(chunks - 1)
+    add_and_send(chunks - 2)
     one.wait_recv()
     for t in range(4):
         total = dt[pl.ds(pl.multiple_of(t * 128 + 64 * core, 64), 64), :] + t1r[t].astype(F32)
-        t2u[yl, t] = total[:, :512].astype(BF)
-        t2s[t] = total[:, 512:].astype(BF)
-    two = copy(t2s, t2u.at[yl], st.at[1], rt.at[1], y_id)
-    two.start()
-    finish(chunks - 2)
-    two.wait_recv()
+        t2s[t, yl] = total[:, :512].astype(BF)
+        t2s[t, 1 - yl] = total[:, 512:].astype(BF)
     me = yh * 4 + z
     three = []
     for d, (a, b) in enumerate(peers):
-        src = t2u.at[lax.rem(b, 2), 2 * a + lax.div(b, 2)]
-        three.append(copy(src, t3r.at[me], st.at[2 + d], rt.at[2 + d], peer_ids[d]))
+        src = t2s.at[2 * a + lax.div(b, 2), lax.rem(b, 2)]
+        three.append(copy(src, t3r.at[me], st.at[1 + d], rt.at[1 + d], peer_ids[d]))
         three[-1].start()
-    t3r[me] = t2u[lax.rem(z, 2), 2 * yh + lax.div(z, 2)]
-    finish(chunks - 1)
+    t3r[me] = t2s[2 * yh + lax.div(z, 2), lax.rem(z, 2)]
+    finish_range(chunks - LAG, chunks - LAG + 2)
+    add_and_send(chunks - 1)
+    finish_range(chunks - LAG + 2, chunks - LAG + 5)
     for one_copy in three:
         one_copy.wait_recv()
     total = t3r[0].astype(F32)
@@ -275,11 +329,26 @@
         t4s[t] = total[:, t * 128 : t * 128 + 128].astype(BF)
     four = []
     for d in range(3):
-        four.append(copy(t4s.at[xs[d]], t4r.at[x], st.at[9 + d], rt.at[9 + d], x_ids[d]))
+        four.append(copy(t4s.at[xs[d]], t4r.at[x], st.at[8 + d], rt.at[8 + d], last_ids[d]))
         four[-1].start()
-    t4r[x] = t4s[x]
+    twin = copy(t4s.at[x], t4r.at[x], st.at[11], rt.at[11], twin_id)
+
+    @pl.when(swaps)
+    def _():
+        twin.start()
+
+    @pl.when(jnp.logical_not(swaps))
+    def _():
+        t4r[x] = t4s[x]
+
+    finish_range(chunks - LAG + 5, chunks)
     for one_copy in four:
         one_copy.wait_recv()
+
+    @pl.when(swaps)
+    def _():
+        twin.wait()
+
     for h in range(HEADS):
         db[h] = t4r[h].astype(F32)
 
@@ -287,29 +356,46 @@
         for d in range(3):
             in_copy(n, d).wait_send()
             out_copy(n, d).wait_send()
-        y_copy(n).wait_send()
+            y_copy(n, d).wait_send()
+        y_own(n).wait_send()
         back_copy(n).wait_send()
         return 0
 
     lax.fori_loop(0, chunks, drain, 0)
     for d in range(3):
         bias_copy(d).wait_send()
-    for one_copy in [one, two] + three + four:
+        bias_twin(d).wait_send()
+    for one_copy in [one] + three + four:
         one_copy.wait_send()
+
+
+def store(*refs):
+    sems = refs[-1]
+    count = (len(refs) - 1) // 2
+    copies = [pltpu.make_async_copy(refs[t], refs[count + t], sems.at[t]) for t in range(count)]
+    for one in copies:
+        one.start()
+    for one in copies:
+        one.wait()
 
 
 def on_device(query, key, value, gate, d_out, bias, length):
     rows = query.shape[0]
     chunks = rows // CI
     vmem = pl.BlockSpec(memory_space=pltpu.VMEM)
+    anywhere = pl.BlockSpec(memory_space=pl.ANY)
     pair = jax.ShapeDtypeStruct(query.shape, BF)
     dma = pltpu.SemaphoreType.DMA
+    shapes = [pair, pair, pair, pair, jax.ShapeDtypeStruct((HEADS, 64, 128), F32)]
     out = pl.pallas_call(
         kernel,
-        out_shape=[pair, pair, pair, pair, jax.ShapeDtypeStruct((HEADS, 64, 128), F32)],
-        in_specs=[vmem] * 6 + [pl.BlockSpec(memory_space=pltpu.SMEM)],
+        out_shape=[pltpu.VMEM(one.shape, one.dtype) for one in shapes],
+        in_specs=[anywhere] * 6 + [pl.BlockSpec(memory_space=pltpu.SMEM)],
         out_specs=[vmem] * 5,
-        scratch_shapes=[
+        scratch_shapes=[pltpu.VMEM(query.shape, BF)] * 5
+        + [
+            pltpu.VMEM(bias.shape, BF),
+            dma((11,)),
             pltpu.VMEM((rows, 4, 4, C, 128), BF),
             pltpu.VMEM((rows, 4, 4, C, 128), BF),
             pltpu.VMEM((rows, 4, 2, C, 128), BF),
@@ -329,22 +415,29 @@
             pltpu.VMEM((512, 1024), F32),
             pltpu.VMEM((4, 64, 1024), BF),
             pltpu.VMEM((4, 64, 1024), BF),
-            pltpu.VMEM((4, 64, 512), BF),
-            pltpu.VMEM((2, 4, 64, 512), BF),
+            pltpu.VMEM((4, 2, 64, 512), BF),
             pltpu.VMEM((8, 64, 512), BF),
             pltpu.VMEM((4, 64, 128), BF),
             pltpu.VMEM((4, 64, 128), BF),
             dma((chunks, 3)), dma((chunks, 3)),
-            dma((chunks,)), dma((chunks,)),
+            dma((chunks, 4)), dma((chunks, 4)),
             dma((chunks,)), dma((chunks,)),
             dma((chunks, 3)), dma((chunks, 3)),
-            dma((3,)), dma((3,)),
+            dma((6,)), dma((6,)),
             dma((12,)), dma((12,)),
         ],
         compiler_params=pltpu.CompilerParams(
-            collective_id=0, has_side_effects=True, vmem_limit_bytes=60 * 2**20
+            collective_id=0, has_side_effects=True, vmem_limit_bytes=56 * 2**20
         ),
     )(query, key, value, gate, d_out, bias, length)
+    out = pl.pallas_call(
+        store,
+        out_shape=shapes,
+        in_specs=[vmem] * 5,
+        out_specs=[anywhere] * 5,
+        scratch_shapes=[dma((5,))],
+        compiler_params=pltpu.CompilerParams(vmem_limit_bytes=6 * 2**20),
+    )(*out)
     return tuple(out)
 
 

time: 146 us -> 103 us (0.71); the launches traced: 144 us -> 103 us
  Pallas kernels: 136 us -> 102 us
  local copies, waits for them, and re-layouts: 6.67 us -> 0 us
    pallas_call x1 -> x2, Pallas kernels: 136 us -> 102 us  [the longest x1 99.9 us: on_device(): pl.pallas_call(kernel, out_shape=[pltpu.VMEM(one.shape, one.dtype) for on...]
    unnamed x13 -> x0, local copies, waits for them, and re-layouts: 6.67 us -> none
where the time goes in v2:
time: 103 us
  Pallas kernels  102 us (99%)
  between operations  1.29 us (1%)
    pallas_call x1, Pallas kernels, on_device(): pl.pallas_call(kernel, out_shape=[pltpu.VMEM(one.shape, one.dtype) for on...  99.9 us

profile of v2, /device:TPU:1, one launch (start us, length us, event | category | flops | bytes accessed | tf_op | source)
XLA Modules:
  0.0 102.9 jit_solution(2477349446197536499)
XLA Ops:
  1.3 99.9 %shard_map.110 = (bf16[24,128,128]{2,1,0:T(8,128)(2,1)S(1)}, bf16[24,128,128]{2,1,0:T(8,128)(2,1)S(1)}, bf16[24,128,128]{2,1,0:T(8,128)(2,1)S(1)}, bf16[24,128,128]{2,1,0:T(8,128)(2,1)S(1)}, f32[4,64,128]{2,1,0:T(8,128)S(1)}) custom-call(bf16[24,128,128]{2,1,0:T(8,128)(2,1)} %q_hbm.1, bf16[24,128,128]{2,1,0:T(8,128)(2,1)} %k_hbm.1, ...), custom_call_target="tpu_custom_call" | custom-call | tf_op jit(solution)/shard_map/pallas_call | solution.py:390
  101.2 1.7 %shard_map.111 = (bf16[24,128,128]{2,1,0:T(8,128)(2,1)}, bf16[24,128,128]{2,1,0:T(8,128)(2,1)}, bf16[24,128,128]{2,1,0:T(8,128)(2,1)}, bf16[24,128,128]{2,1,0:T(8,128)(2,1)}, f32[4,64,128]{2,1,0:T(8,128)}) custom-call(bf16[24,128,128]{2,1,0:T(8,128)(2,1)S(1)} %get-tuple-element.10.refs_0_, bf16[24,128,128]{2,1,0:T(8,128)(2,1)S(1)} %get-tuple-element.11.refs_1_, ...), custom_call_target="tpu_custom_call" | custom-call | tf_op jit(solution)/shard_map/pallas_call | solution.py:433

commit v3 on v2

--- a/solution.py
+++ b/solution.py
@@ -170,7 +170,7 @@
             rx[i, x] = snd[i, x]
 
     def send_in(n):
-        for d in range(3):
+        for d in (1, 0, 2):
             in_copy(n, d).start()
         y_own(n).start()
 
@@ -181,7 +181,7 @@
         return 0
 
     def forwarded(n):
-        return jnp.minimum(chunks, 2 + n + lax.div(n, 3))
+        return jnp.minimum(chunks, 2 + n)
 
     for one_load in loads[:5]:
         one_load.wait()
@@ -304,7 +304,6 @@
         t1s[t] = dt[pl.ds(pl.multiple_of(t * 128 + 64 * (1 - core), 64), 64), :].astype(BF)
     one = copy(t1s, t1r, st.at[0], rt.at[0], core_id)
     one.start()
-    add_and_send(chunks - 2)
     one.wait_recv()
     for t in range(4):
         total = dt[pl.ds(pl.multiple_of(t * 128 + 64 * core, 64), 64), :] + t1r[t].astype(F32)
@@ -317,9 +316,9 @@
         three.append(copy(src, t3r.at[me], st.at[1 + d], rt.at[1 + d], peer_ids[d]))
         three[-1].start()
     t3r[me] = t2s[2 * yh + lax.div(z, 2), lax.rem(z, 2)]
-    finish_range(chunks - LAG, chunks - LAG + 2)
+    add_and_send(chunks - 2)
     add_and_send(chunks - 1)
-    finish_range(chunks - LAG + 2, chunks - LAG + 5)
+    finish_range(chunks - LAG, chunks - LAG + 5)
     for one_copy in three:
         one_copy.wait_recv()
     total = t3r[0].astype(F32)

time: 103 us -> 101 us (0.981)
  Pallas kernels: 102 us -> 99.3 us
    pallas_call x1, Pallas kernels: 99.9 us -> 97.6 us  [on_device(): pl.pallas_call(kernel, out_shape=[pltpu.VMEM(one.shape, one.dtype) for on...]
where the time goes in v3:
time: 101 us
  Pallas kernels  99.3 us (98%)
  between operations  1.29 us (1%)
    pallas_call x1, Pallas kernels, on_device(): pl.pallas_call(kernel, out_shape=[pltpu.VMEM(one.shape, one.dtype) for on...  97.6 us

profile of v3, /device:TPU:1, one launch (start us, length us, event | category | flops | bytes accessed | tf_op | source)
XLA Modules:
  0.0 100.6 jit_solution(17745072209360628897)
XLA Ops:
  1.3 97.6 %shard_map.110 = (bf16[24,128,128]{2,1,0:T(8,128)(2,1)S(1)}, bf16[24,128,128]{2,1,0:T(8,128)(2,1)S(1)}, bf16[24,128,128]{2,1,0:T(8,128)(2,1)S(1)}, bf16[24,128,128]{2,1,0:T(8,128)(2,1)S(1)}, f32[4,64,128]{2,1,0:T(8,128)S(1)}) custom-call(bf16[24,128,128]{2,1,0:T(8,128)(2,1)} %q_hbm.1, bf16[24,128,128]{2,1,0:T(8,128)(2,1)} %k_hbm.1, ...), custom_call_target="tpu_custom_call" | custom-call | tf_op jit(solution)/shard_map/pallas_call | solution.py:389
  98.9 1.7 %shard_map.111 = (bf16[24,128,128]{2,1,0:T(8,128)(2,1)}, bf16[24,128,128]{2,1,0:T(8,128)(2,1)}, bf16[24,128,128]{2,1,0:T(8,128)(2,1)}, bf16[24,128,128]{2,1,0:T(8,128)(2,1)}, f32[4,64,128]{2,1,0:T(8,128)}) custom-call(bf16[24,128,128]{2,1,0:T(8,128)(2,1)S(1)} %get-tuple-element.10.refs_0_, bf16[24,128,128]{2,1,0:T(8,128)(2,1)S(1)} %get-tuple-element.11.refs_1_, ...), custom_call_target="tpu_custom_call" | custom-call | tf_op jit(solution)/shard_map/pallas_call | solution.py:432

commit v4 on v3

--- a/solution.py
+++ b/solution.py
@@ -16,7 +16,7 @@
 SCALE = C**-0.5
 LOG2E = math.log2(math.e)
 CI = 2
-LAG = 8
+LAG = 6
 ADD = 2
 KC = 256
 NN = (((1,), (0,)), ((), ()))

time: 101 us -> 101 us (level)
  no operation moved by 1% of the time
where the time goes in v4:
time: 101 us
  Pallas kernels  99.3 us (98%)
  between operations  1.29 us (1%)
    pallas_call x1, Pallas kernels, on_device(): pl.pallas_call(kernel, out_shape=[pltpu.VMEM(one.shape, one.dtype) for on...  97.6 us

profile of v4, /device:TPU:1, one launch (start us, length us, event | category | flops | bytes accessed | tf_op | source)
XLA Modules:
  0.0 100.6 jit_solution(8827149273177399046)
XLA Ops:
  1.3 97.6 %shard_map.110 = (bf16[24,128,128]{2,1,0:T(8,128)(2,1)S(1)}, bf16[24,128,128]{2,1,0:T(8,128)(2,1)S(1)}, bf16[24,128,128]{2,1,0:T(8,128)(2,1)S(1)}, bf16[24,128,128]{2,1,0:T(8,128)(2,1)S(1)}, f32[4,64,128]{2,1,0:T(8,128)S(1)}) custom-call(bf16[24,128,128]{2,1,0:T(8,128)(2,1)} %q_hbm.1, bf16[24,128,128]{2,1,0:T(8,128)(2,1)} %k_hbm.1, ...), custom_call_target="tpu_custom_call" | custom-call | tf_op jit(solution)/shard_map/pallas_call | solution.py:389
  98.9 1.7 %shard_map.111 = (bf16[24,128,128]{2,1,0:T(8,128)(2,1)}, bf16[24,128,128]{2,1,0:T(8,128)(2,1)}, bf16[24,128,128]{2,1,0:T(8,128)(2,1)}, bf16[24,128,128]{2,1,0:T(8,128)(2,1)}, f32[4,64,128]{2,1,0:T(8,128)}) custom-call(bf16[24,128,128]{2,1,0:T(8,128)(2,1)S(1)} %get-tuple-element.10.refs_0_, bf16[24,128,128]{2,1,0:T(8,128)(2,1)S(1)} %get-tuple-element.11.refs_1_, ...), custom_call_target="tpu_custom_call" | custom-call | tf_op jit(solution)/shard_map/pallas_call | solution.py:432
